TPU v7x, 128 devices: a whole 4x4x4 slice. The times are simulated.
128 devices in a mesh: expert: 32 (over y, z, core), vocab: 4 (over x).
Axes of the slice: x: 4, y: 4, z: 4, core: 2. Of those that a mesh axis runs over, the one named last changes fastest.
Arguments:
- tokens: bfloat16 [4096, 2048], P('expert'), may hold values from -12 to 12
- expert_ids: int32 [4096, 6], P('expert'), may hold values from 0 to 63, all different within a row; in each aligned block of 128 rows (0 to 127, 128 to 255, ...) at most 24 rows name the same one
- gates: float32 [4096, 6], P('expert'), may hold values from 0.05 to 0.4
- w_gate: bfloat16 [64, 2048, 1408], P('expert', None, 'vocab'), may hold values from -0.125 to 0.125
- w_up: bfloat16 [64, 2048, 1408], P('expert', None, 'vocab'), may hold values from -0.125 to 0.125
- w_down: bfloat16 [64, 1408, 2048], P('expert', 'vocab'), may hold values from -0.21875 to 0.21875
- norm_gain: float32 [2048], replicated, may hold values from 0.5 to 1.5
- lm_weight: bfloat16 [2048, 98304], P(None, ('expert', 'vocab')), may hold values from -6.9605824 to 6.9605824
- targets: int32 [4096], P('expert'), may hold values from 0 to 98303
Outputs:
- logprobs: float32 [4096], P('expert')
Inputs may be any that keep to these rules, and one draw needn't show every extreme that they name: `expert_ids`: in the 128 rows of one device no expert is named by more than 24 routes; each row names 6 different experts.
All inputs are finite; a program needn't handle non-finite values.
Results may differ from a plain program's by a relative error of at most 0.003.
Values may be sent and summed in bfloat16 or wider, within the bound.
A program may use at most 128 MiB of HBM per device.

v0:
```python
import jax
import jax.numpy as jnp
from jax import lax
from jax.sharding import PartitionSpec as P


def split_up(array, dim, count):
    before, after = (array.shape[:dim], array.shape[dim + 1 :])
    return jnp.moveaxis(array.reshape(*before, count, -1, *after), dim, 0)


def piece_ends(length, count):
    unit = 8 if length >= 8 * count else 1
    return [length // unit * k // count * unit for k in range(1, count)]


def laid_out(parts, dim):
    shape = list(parts.shape[1:])
    shape[dim] *= parts.shape[0]
    return jnp.moveaxis(parts, 0, dim).reshape(shape)


def several_exchanges(array, axis, pieces, split_dim, concat_dim):
    parts = split_up(array, split_dim, lax.axis_size(axis))
    widest = max(range(1, max(2, parts.ndim - 1)), key=lambda d: parts.shape[d])
    done = []
    for share in jnp.split(parts, piece_ends(parts.shape[widest], pieces), axis=widest):
        if share.size:
            done.append(lax.all_to_all(share, axis, split_axis=0, concat_axis=0, tiled=True))
    return laid_out(jnp.concatenate(done, axis=widest), concat_dim)


def copy_for_each(array, axis):
    count = lax.axis_size(axis)
    return lax.all_to_all(
        jnp.broadcast_to(array[None], (count, *array.shape)), axis, 0, 0, tiled=True
    )


def taken_together(array, axis):
    everything = copy_for_each(array, axis)
    return jnp.sum(everything, axis=0)


def gathered_once(array, axis):
    leaves = jax.tree.leaves(array)
    turns = sorted(range(len(leaves)), key=lambda k: -leaves[k].size)
    width = (1, *leaves[turns[0]].shape)[-1]
    lines = [
        jnp.pad(leaves[k].reshape(-1), (0, -leaves[k].size % width)).reshape(-1, width)
        for k in turns
    ]
    both, at, found = (copy_for_each(jnp.concatenate(lines), axis), 0, {})
    for k, line in zip(turns, lines):
        share = both[:, at : at + len(line)].reshape(len(both), -1)
        found[k] = share[:, : leaves[k].size].reshape(-1, *leaves[k].shape)
        at += len(line)
    numbers = iter(range(len(leaves)))
    return jax.tree.map(lambda _: found[next(numbers)], array)


def joined_by_halves(pieces, combine):
    while len(jax.tree.leaves(pieces)[0]) > 1:
        pieces = jax.vmap(combine)(
            *(jax.tree.map(lambda part: part[side::2], pieces) for side in (0, 1))
        )
    return jax.tree.map(lambda part: part[0], pieces)


def joined_all(array, axis, combine):
    pieces = gathered_once(array, axis)
    return joined_by_halves(pieces, combine)


def expert_rows(received, w_gate, w_up, w_down):
    groups = w_gate.shape[0]
    shaped = received.reshape(-1, groups, received.shape[1], received.shape[2])
    gate_val = jnp.einsum("sltd,ldf->sltf", shaped, w_gate, preferred_element_type=jnp.float32)
    up_val = jnp.einsum("sltd,ldf->sltf", shaped, w_up, preferred_element_type=jnp.float32)
    hidden = (jax.nn.silu(gate_val) * up_val).astype(jnp.bfloat16)
    result = jnp.einsum("sltf,lfd->sltd", hidden, w_down, preferred_element_type=jnp.float32)
    return result.reshape(received.shape[0], received.shape[1], result.shape[3])


def shard_stats(logits, row_targets, base):
    columns = base + jnp.arange(logits.shape[1], dtype=jnp.int32)
    top_now = jnp.max(logits, axis=1)
    total_now = jnp.sum(jnp.exp(logits - top_now[:, None]), axis=1)
    picked_now = jnp.sum(jnp.where(columns[None, :] == row_targets[:, None], logits, 0.0), axis=1)
    return (top_now, total_now, picked_now)


def join_stats(first, second):
    best = jnp.maximum(first[0], second[0])
    mass = first[1] * jnp.exp(first[0] - best) + second[1] * jnp.exp(second[0] - best)
    return (best, mass, first[2] + second[2])


def body(tokens, expert_ids, gates, w_gate, w_up, w_down, norm_gain, lm_weight, targets):
    tok_rows = tokens.shape[0]
    top_count = expert_ids.shape[1]
    groups = w_gate.shape[0]
    width = tokens.shape[1]
    expert_devs = lax.axis_size("expert")
    vocab_devs = lax.axis_size("vocab")
    experts_all = groups * expert_devs
    slots = 2 * tok_rows * top_count // experts_all
    vocab_index = lax.axis_index("vocab")
    flat_ids = expert_ids.reshape(-1)
    onehot = (flat_ids[:, None] == jnp.arange(experts_all, dtype=jnp.int32)[None, :]).astype(
        jnp.int32
    )
    slot_ids = jnp.sum((jnp.cumsum(onehot, axis=0) - onehot) * onehot, axis=1)
    target_rows = (flat_ids * slots + slot_ids).reshape(tok_rows, top_count)
    places = jnp.arange(experts_all * slots, dtype=jnp.int32)
    packed = jnp.dot(
        jnp.any(places[:, None, None] == target_rows[None, :, :], axis=2).astype(jnp.bfloat16),
        tokens,
        preferred_element_type=jnp.float32,
    ).astype(jnp.bfloat16)
    packed = packed.reshape(experts_all, slots, width)
    partial_value = expert_rows(
        lax.all_to_all(packed, "expert", split_axis=0, concat_axis=0, tiled=True),
        w_gate,
        w_up,
        w_down,
    )
    combined = several_exchanges(partial_value, "expert", 2, 0, 0)
    flat_back = combined.reshape(experts_all * slots, combined.shape[2])
    picked = jnp.take(flat_back, target_rows.reshape(-1), axis=0).reshape(
        tok_rows, top_count, flat_back.shape[1]
    )
    mixture = jnp.sum(picked * gates[:, :, None], axis=1)
    base = (lax.axis_index("expert") * vocab_devs + vocab_index) * lm_weight.shape[1]
    mixture = taken_together(mixture, "vocab")
    resid = (tokens.astype(jnp.float32) + mixture).astype(jnp.bfloat16)
    resid_f = resid.astype(jnp.float32)
    squares = jnp.mean(resid_f * resid_f, axis=1)
    normed = (resid_f * lax.rsqrt(squares + 1e-06)[:, None] * norm_gain[None, :]).astype(
        jnp.bfloat16
    )
    rows = lax.all_gather(normed, "expert", axis=0, tiled=True)
    row_targets = lax.all_gather(targets, "expert", axis=0, tiled=True)
    logits = jnp.dot(rows, lm_weight, preferred_element_type=jnp.float32)
    fresh = shard_stats(logits, row_targets, base)
    top_all, total_all, chosen_all = tuple((new for new in fresh))
    top_got, total_got, chosen_got = (
        lax.all_to_all(top_all, "expert", split_axis=0, concat_axis=0, tiled=True),
        lax.all_to_all(total_all, "expert", split_axis=0, concat_axis=0, tiled=True),
        lax.all_to_all(chosen_all, "expert", split_axis=0, concat_axis=0, tiled=True),
    )
    top_got = top_got.reshape(expert_devs, tok_rows)
    total_got = total_got.reshape(expert_devs, tok_rows)
    chosen_got = chosen_got.reshape(expert_devs, tok_rows)
    best = jnp.max(top_got, axis=0)
    mass = jnp.sum(total_got * jnp.exp(top_got - best[None, :]), axis=0)
    chosen = jnp.sum(chosen_got, axis=0)
    best, mass, chosen = joined_all((best, mass, chosen), "vocab", join_stats)
    return chosen - best - jnp.log(mass)


def solution(mesh):
    in_specs = (
        P("expert", None),
        P("expert", None),
        P("expert", None),
        P("expert", None, "vocab"),
        P("expert", None, "vocab"),
        P("expert", "vocab", None),
        P(),
        P(None, ("expert", "vocab")),
        P("expert"),
    )
    out_specs = P("expert")
    return jax.shard_map(body, mesh=mesh, in_specs=in_specs, out_specs=out_specs, check_vma=False)
```

profile of v0, /device:TPU:0, one launch (start us, length us, event | category | flops | bytes accessed | tf_op | source)
XLA Modules:
  0.0 552.3 jit_solution(4479632245104566551)
XLA Ops:
  14.6 81.5 %all_to_all.52 = bf16[64,24,2048]{2,1,0:T(8,128)(2,1)S(1)} all-to-all(bf16[64,24,2048]{2,1,0:T(8,128)(2,1)S(1)} %bitcast.93), channel_id=1, replica_groups=mesh['expert'=32,'vocab'=4] {'expert'}, dimensions={0} | all-to-all | bytes 12582912 | tf_op jit(solution)/shard_map/all_to_all | solution.py:123
  98.7 4.9 fusion.2
  103.5 13.6 %convolution_bitcast_fusion = f32[32,2,24,2048]{3,2,0,1:T(8,128)} fusion(bf16[2,352,2048]{2,1,0:T(8,128)(2,1)} %param.14, f32[2,32,24,352]{3,2,1,0:T(8,128)} %fusion.2, bf16[2,2048,352]{1,2,0:T(8,128)(2,1)} %param.13, bf16[32,2,24,2048]{3,2,1,0:T(8,128)(2,1)} %bitcast.95), kind=kOutput, calls=%fused_computation.10 | convolution fusion | flops 4432429056 | bytes 26804224 | tf_op jit(solution)/shard_map/sltf,lfd->sltd/dot_general | solution.py:81
  121.5 4.9 all-to-all-start.1
  129.8 3.8 copy.55
  133.6 45.4 %all-to-all-done.1 = f32[32,2,8,2048]{3,2,1,0:T(8,128)} async-done(((f32[32,2,8,2048]{3,2,1,0:T(8,128)}), f32[32,2,8,2048]{3,2,1,0:T(8,128)}, u32[]{:S(2)}, u32[]{:S(2)}) %all-to-all-start.1) | async-done | bytes 4194336 | tf_op jit(solution)/shard_map/all_to_all | solution.py:29
  178.9 6.8 %all-to-all-start.2 = ((f32[32,2,16,2048]{3,2,1,0:T(8,128)}), f32[32,2,16,2048]{3,2,1,0:T(8,128)}, u32[]{:S(2)}, u32[]{:S(2)}) async-start(f32[32,2,16,2048]{3,2,1,0:T(8,128)} %copy.55), calls=%async_computation.2 | async-start | bytes 16777216 | tf_op jit(solution)/shard_map/all_to_all | solution.py:29
  186.4 112.9 %all-to-all-done.2 = f32[32,2,16,2048]{3,2,1,0:T(8,128)} async-done(((f32[32,2,16,2048]{3,2,1,0:T(8,128)}), f32[32,2,16,2048]{3,2,1,0:T(8,128)}, u32[]{:S(2)}, u32[]{:S(2)}) %all-to-all-start.2) | async-done | bytes 8388640 | tf_op jit(solution)/shard_map/all_to_all | solution.py:29
  299.3 11.3 %pad_maximum_fusion = f32[32,2,24,2048]{3,2,1,0:T(8,128)} fusion(f32[32,2,16,2048]{3,2,1,0:T(8,128)} %all-to-all-done.2, f32[32,2,8,2048]{3,2,1,0:T(8,128)} %all-to-all-done.1), kind=kLoop, calls=%fused_computation.1 | loop fusion | flops 3145728 | bytes 25165824 | tf_op jit(solution)/shard_map/concatenate | solution.py:30
  310.6 11.8 %gather_fusion = f32[768,2048]{1,0:T(8,128)} fusion(f32[1536,2048]{1,0:T(8,128)} %bitcast.92, s32[1024]{0:T(1024)S(1)} %pad_clamp_fusion), kind=kCustom, calls=%fused_computation | custom fusion | bytes 12585984 | tf_op jit(solution)/shard_map/jit(_take)/gather | solution.py:130
  322.4 7.8 %gather.7 = f32[128,6,2048]{2,1,0:T(8,128)} reshape(f32[768,2048]{1,0:T(8,128)} %gather_fusion) | data formatting | bytes 12582912 | tf_op jit(solution)/shard_map/jit(_take)/gather | solution.py:130
  330.3 6.5 %multiply_reduce_fusion = f32[128,2048]{1,0:T(8,128)S(1)} fusion(f32[128,6,2048]{2,1,0:T(8,128)} %gather.7, f32[128,6]{1,0:T(8,128)S(1)} %copy.57, pred[128,6]{1,0:T(8,128)(4,1)S(1)} %copy.51), kind=kLoop, calls=%fused_computation.4 | loop fusion | flops 4456448 | bytes 7343872 | tf_op jit(solution)/shard_map/reduce_sum | solution.py:133
  337.3 47.0 %all_to_all.53 = f32[4,128,2048]{2,1,0:T(8,128)} all-to-all(f32[4,128,2048]{2,1,0:T(8,128)S(1)} %broadcast_in_dim.20), channel_id=1, replica_groups=mesh['expert'=32,'vocab'=4] {'vocab'}, dimensions={0} | all-to-all | bytes 8388608 | tf_op jit(solution)/shard_map/all_to_all | solution.py:35
  384.3 3.6 reduce_sum.80
  391.9 37.4 %all-gather = s32[32,1,128]{2,1,0:T(1,128)S(1)} all-gather(s32[1,1,128]{2,1,0:T(1,128)S(1)} %bitcast.109), channel_id=1, replica_groups=mesh['expert'=32,'vocab'=4] {'expert'}, dimensions={0}, use_global_device_ids=true | all-gather | bytes 16896 | tf_op jit(solution)/shard_map/all_gather | solution.py:143
  429.3 47.4 %all-gather.3.cloned.1.call-done = bf16[4096,2048]{1,0:T(8,128)(2,1)} async-done(((bf16[128,2048]{1,0:T(8,128)(2,1)}), bf16[4096,2048]{1,0:T(8,128)(2,1)}) %all-gather.3.cloned.1.call-update) | async-done | bytes 16777232 | tf_op jit(solution)/shard_map/all_gather | solution.py:142
  476.7 20.1 %fusion.33 = (f32[4096]{0:T(1024)}, f32[4096,768]{0,1:T(8,128)}) fusion(bf16[4096,2048]{1,0:T(8,128)(2,1)} %all-gather.3.cloned.1.call-done, bf16[2048,768]{1,0:T(8,128)(2,1)S(1)} %copy-done), kind=kOutput, calls=%fused_computation.55 | convolution fusion | flops 12888043520 | bytes 32522240 | tf_op jit(solution)/shard_map/dot_general | solution.py:144
  496.8 5.4 all-to-all-start.4
  502.2 7.2 %exponential_reduce_fusion = (f32[4096]{0:T(1024)}, f32[4096]{0:T(1024)}) fusion(f32[4096,768]{0,1:T(8,128)} %get-tuple-element.15, f32[4096]{0:T(1024)} %get-tuple-element.14, s32[4096]{0:T(1024)S(1)} %bitcast.97, s32[768]{0:T(1024)S(1)} %iota_add_fusion), kind=kLoop, calls=%fused_computation.3 | loop fusion | flops 15720448 | bytes 12651520 | tf_op jit(solution)/shard_map/reduce_sum | solution.py:88
  509.6 7.2 %all-to-all-start.5 = ((f32[32,128,1]{1,2,0:T(1,128)}), f32[32,128,1]{1,2,0:T(1,128)S(1)}, u32[]{:S(2)}, u32[]{:S(2)}) async-start(f32[32,128,1]{1,2,0:T(1,128)} %bitcast.16), calls=%async_computation.5 | async-start | bytes 32768 | tf_op jit(solution)/shard_map/all_to_all | solution.py:149
  516.9 7.3 %all-to-all-done.5 = f32[32,128,1]{1,2,0:T(1,128)S(1)} async-done(((f32[32,128,1]{1,2,0:T(1,128)}), f32[32,128,1]{1,2,0:T(1,128)S(1)}, u32[]{:S(2)}, u32[]{:S(2)}) %all-to-all-start.5) | async-done | bytes 16416 | tf_op jit(solution)/shard_map/all_to_all | solution.py:149
  524.2 3.8 all-to-all-start.6
  528.0 7.3 %all-to-all-done.6 = f32[32,128,1]{1,2,0:T(1,128)S(1)} async-done(((f32[32,128,1]{1,2,0:T(1,128)}), f32[32,128,1]{1,2,0:T(1,128)S(1)}, u32[]{:S(2)}, u32[]{:S(2)}) %all-to-all-start.6) | async-done | bytes 16416 | tf_op jit(solution)/shard_map/all_to_all | solution.py:150
  535.4 9.4 %all_to_all.54 = f32[4,3,128]{2,1,0:T(4,128)S(1)} all-to-all(f32[4,3,128]{2,1,0:T(4,128)S(1)} %broadcast_in_dim.22), channel_id=1, replica_groups=mesh['expert'=32,'vocab'=4] {'vocab'}, dimensions={0} | all-to-all | bytes 12288 | tf_op jit(solution)/shard_map/all_to_all | solution.py:35
  (62 shorter events, 24.5 us)
Async XLA Ops:
  6.5 470.2 %copy-start = (bf16[2048,768]{1,0:T(8,128)(2,1)S(1)}, bf16[2048,768]{1,0:T(8,128)(2,1)}, u32[]{:S(2)}) copy-start(bf16[2048,768]{1,0:T(8,128)(2,1)} %param.16) | copy-start | bytes 9437188
  14.6 84.1 %copy-start.6 = (bf16[2,2048,352]{1,2,0:T(8,128)(2,1)S(1)}, bf16[2,2048,352]{1,2,0:T(8,128)(2,1)}, u32[]{:S(2)}) copy-start(bf16[2,2048,352]{1,2,0:T(8,128)(2,1)} %param.12) | copy-start | bytes 8650756
  96.1 2.6 copy-start.1
  117.1 2.2 slice-start
  121.5 57.4 %all-to-all-start.1 = ((f32[32,2,8,2048]{3,2,1,0:T(8,128)}), f32[32,2,8,2048]{3,2,1,0:T(8,128)}, u32[]{:S(2)}, u32[]{:S(2)}) async-start(f32[32,2,8,2048]{3,2,1,0:T(8,128)} %copy.54), calls=%async_computation.1 | async-start | bytes 8388608 | tf_op jit(solution)/shard_map/all_to_all | solution.py:29
  126.4 3.4 slice-start.1
  133.6 52.2 %copy-start.2 = (s32[128,6]{0,1:T(8,128)S(1)}, s32[128,6]{0,1:T(8,128)}, u32[]{:S(2)}) copy-start(s32[128,6]{0,1:T(8,128)} %param.10) | copy-start | bytes 9220
  133.6 52.7 %copy-start.4 = (f32[128,6]{0,1:T(8,128)S(1)}, f32[128,6]{0,1:T(8,128)}, u32[]{:S(2)}) copy-start(f32[128,6]{0,1:T(8,128)} %param.11) | copy-start | bytes 9220
  178.9 120.3 %all-to-all-start.2 = ((f32[32,2,16,2048]{3,2,1,0:T(8,128)}), f32[32,2,16,2048]{3,2,1,0:T(8,128)}, u32[]{:S(2)}, u32[]{:S(2)}) async-start(f32[32,2,16,2048]{3,2,1,0:T(8,128)} %copy.55), calls=%async_computation.2 | async-start | bytes 16777216 | tf_op jit(solution)/shard_map/all_to_all | solution.py:29
  185.8 290.9 %all-gather.3.cloned.1.call-start = ((), (), s32[]{:S(2)}) async-start(), calls=%async_computation.8 | async-start | bytes 17301504 | tf_op jit(solution)/shard_map/all_gather | solution.py:142
  337.3 52.2 %copy-start.3 = (f32[2048]{0:T(1024)S(1)}, f32[2048]{0:T(1024)}, u32[]{:S(2)}) copy-start(f32[2048]{0:T(1024)} %param.15) | copy-start | bytes 24580
  384.3 7.5 %copy-start.5 = (s32[128]{0:T(128)S(1)}, s32[128]{0:T(128)}, u32[]{:S(2)}) copy-start(s32[128]{0:T(128)} %param.17) | copy-start | bytes 1540
  496.8 12.8 %all-to-all-start.4 = ((f32[32,128,1]{1,2,0:T(1,128)}), f32[32,128,1]{1,2,0:T(1,128)S(1)}, u32[]{:S(2)}, u32[]{:S(2)}) async-start(f32[32,128,1]{1,2,0:T(1,128)} %bitcast.14), calls=%async_computation.4 | async-start | bytes 32768 | tf_op jit(solution)/shard_map/all_to_all | solution.py:148
  509.6 14.6 %all-to-all-start.5 = ((f32[32,128,1]{1,2,0:T(1,128)}), f32[32,128,1]{1,2,0:T(1,128)S(1)}, u32[]{:S(2)}, u32[]{:S(2)}) async-start(f32[32,128,1]{1,2,0:T(1,128)} %bitcast.16), calls=%async_computation.5 | async-start | bytes 32768 | tf_op jit(solution)/shard_map/all_to_all | solution.py:149
  524.2 11.2 %all-to-all-start.6 = ((f32[32,128,1]{1,2,0:T(1,128)}), f32[32,128,1]{1,2,0:T(1,128)S(1)}, u32[]{:S(2)}, u32[]{:S(2)}) async-start(f32[32,128,1]{1,2,0:T(1,128)} %bitcast.23), calls=%async_computation.6 | async-start | bytes 32768 | tf_op jit(solution)/shard_map/all_to_all | solution.py:150
Sparse Core Ops, SparseCore 0:
  392.0 84.6 all-gather.2
where the time goes:
time: 553 us; the launch traced here: 552 us
  waiting for transfers between devices  221 us (40%)
  blocking collectives  175 us (32%)
  matrix products  41.4 us (7%)
  local copies, waits for them, and re-layouts  36.7 us (7%)
  other arithmetic  36.7 us (7%)
  starting transfers between devices  28.1 us (5%)
  between operations  13.6 us (2%)
    all_to_all x2, waiting for transfers between devices, several_exchanges(): lax.all_to_all(share, axis, split_axis=0, concat_axis=0, tiled=True)  158 us
    all_to_all x1, blocking collectives, body(): lax.all_to_all(packed, 'expert', split_axis=0, concat_axis=0, tiled=True)  81.5 us
    all_to_all x2, blocking collectives, copy_for_each(): lax.all_to_all(jnp.broadcast_to(array[None], (count, *array.shape)), axis...  56.4 us
    all_gather x1, waiting for transfers between devices, body(): rows = lax.all_gather(normed, 'expert', axis=0, tiled=True)  47.4 us
    all_gather x1, blocking collectives, body(): row_targets = lax.all_gather(targets, 'expert', axis=0, tiled=True)  37.4 us
    dot_general x1, matrix products, body(): logits = jnp.dot(rows, lm_weight, preferred_element_type=jnp.float32)  20.1 us
    gather x2, local copies, waits for them, and re-layouts, body(): jnp.take(flat_back, target_rows.reshape(-1), axis=0)  19.6 us
    dot_general x1, matrix products, expert_rows(): jnp.einsum('sltf,lfd->sltd', hidden, w_down, preferred_element_type=jnp.f...  13.6 us
  transfers between devices with their start and end apart: 6, of which 6 were waited for; matrix products, arithmetic and copies ran while one was open for 2% of the time, Pallas kernels for 0%

commit v1 on v0

--- a/solution.py
+++ b/solution.py
@@ -140,7 +140,9 @@
         jnp.bfloat16
     )
     rows = lax.all_gather(normed, "expert", axis=0, tiled=True)
-    row_targets = lax.all_gather(targets, "expert", axis=0, tiled=True)
+    row_targets = jnp.concatenate(
+        lax.all_to_all(jnp.stack([targets] * lax.axis_size("expert")), "expert", 0, 0), axis=0
+    )
     logits = jnp.dot(rows, lm_weight, preferred_element_type=jnp.float32)
     fresh = shard_stats(logits, row_targets, base)
     top_all, total_all, chosen_all = tuple((new for new in fresh))

time: 553 us -> 553 us (level)
  blocking collectives: 175 us -> 138 us
  starting transfers between devices: 28.1 us -> 48 us
  waiting for transfers between devices: 221 us -> 237 us
    all_gather x1 -> x0, blocking collectives: 37.4 us -> none  [body(): row_targets = lax.all_gather(targets, 'expert', axis=0, tiled=True)]
    all_to_all x0 -> x1, starting transfers between devices: none -> 19.9 us  [body(): lax.all_to_all(jnp.stack([targets] * lax.axis_size('expert')), 'expert',...]
    all_gather x1, waiting for transfers between devices: 47.4 us -> 64.2 us  [body(): rows = lax.all_gather(normed, 'expert', axis=0, tiled=True)]
  transfers between devices with their start and end apart: 6 -> 7, of which waited for: 6 -> 6; matrix products, arithmetic and copies ran while one was open for 2% -> 6% of each run, Pallas kernels for 0% -> 0%
where the time goes in v1:
time: 553 us; the launch traced here: 552 us
  waiting for transfers between devices  237 us (43%)
  blocking collectives  138 us (25%)
  starting transfers between devices  48 us (9%)
  matrix products  41.4 us (7%)
  local copies, waits for them, and re-layouts  37.3 us (7%)
  other arithmetic  36.7 us (7%)
  between operations  13.6 us (2%)
    all_to_all x2, waiting for transfers between devices, several_exchanges(): lax.all_to_all(share, axis, split_axis=0, concat_axis=0, tiled=True)  158 us
    all_to_all x1, blocking collectives, body(): lax.all_to_all(packed, 'expert', split_axis=0, concat_axis=0, tiled=True)  81.5 us
    all_gather x1, waiting for transfers between devices, body(): rows = lax.all_gather(normed, 'expert', axis=0, tiled=True)  64.2 us
    all_to_all x2, blocking collectives, copy_for_each(): lax.all_to_all(jnp.broadcast_to(array[None], (count, *array.shape)), axis...  56.4 us
    dot_general x1, matrix products, body(): logits = jnp.dot(rows, lm_weight, preferred_element_type=jnp.float32)  20.1 us
    all_to_all x1, starting transfers between devices, body(): lax.all_to_all(jnp.stack([targets] * lax.axis_size('expert')), 'expert',...  19.9 us
    gather x2, local copies, waits for them, and re-layouts, body(): jnp.take(flat_back, target_rows.reshape(-1), axis=0)  19.6 us
    dot_general x1, matrix products, expert_rows(): jnp.einsum('sltf,lfd->sltd', hidden, w_down, preferred_element_type=jnp.f...  13.6 us
  transfers between devices with their start and end apart: 7, of which 6 were waited for; matrix products, arithmetic and copies ran while one was open for 6% of the time, Pallas kernels for 0%

profile of v1, /device:TPU:0, one launch (start us, length us, event | category | flops | bytes accessed | tf_op | source)
XLA Modules:
  0.0 552.2 jit_solution(9565386547470136684)
XLA Ops:
  14.6 81.5 %all_to_all.58 = bf16[64,24,2048]{2,1,0:T(8,128)(2,1)S(1)} all-to-all(bf16[64,24,2048]{2,1,0:T(8,128)(2,1)S(1)} %bitcast.92), channel_id=1, replica_groups=mesh['expert'=32,'vocab'=4] {'expert'}, dimensions={0} | all-to-all | bytes 12582912 | tf_op jit(solution)/shard_map/all_to_all | solution.py:123
  98.7 4.9 fusion.2
  103.5 13.6 %convolution_bitcast_fusion = f32[32,2,24,2048]{3,2,0,1:T(8,128)} fusion(bf16[2,352,2048]{2,1,0:T(8,128)(2,1)} %param.14, f32[2,32,24,352]{3,2,1,0:T(8,128)} %fusion.2, bf16[2,2048,352]{1,2,0:T(8,128)(2,1)} %param.13, bf16[32,2,24,2048]{3,2,1,0:T(8,128)(2,1)} %bitcast.94), kind=kOutput, calls=%fused_computation.10 | convolution fusion | flops 4432429056 | bytes 26804224 | tf_op jit(solution)/shard_map/sltf,lfd->sltd/dot_general | solution.py:81
  121.5 4.9 all-to-all-start.1
  129.8 3.8 copy.55
  133.6 45.4 %all-to-all-done.1 = f32[32,2,8,2048]{3,2,1,0:T(8,128)} async-done(((f32[32,2,8,2048]{3,2,1,0:T(8,128)}), f32[32,2,8,2048]{3,2,1,0:T(8,128)}, u32[]{:S(2)}, u32[]{:S(2)}) %all-to-all-start.1) | async-done | bytes 4194336 | tf_op jit(solution)/shard_map/all_to_all | solution.py:29
  178.9 6.8 %all-to-all-start.2 = ((f32[32,2,16,2048]{3,2,1,0:T(8,128)}), f32[32,2,16,2048]{3,2,1,0:T(8,128)}, u32[]{:S(2)}, u32[]{:S(2)}) async-start(f32[32,2,16,2048]{3,2,1,0:T(8,128)} %copy.55), calls=%async_computation.2 | async-start | bytes 16777216 | tf_op jit(solution)/shard_map/all_to_all | solution.py:29
  186.4 112.9 %all-to-all-done.2 = f32[32,2,16,2048]{3,2,1,0:T(8,128)} async-done(((f32[32,2,16,2048]{3,2,1,0:T(8,128)}), f32[32,2,16,2048]{3,2,1,0:T(8,128)}, u32[]{:S(2)}, u32[]{:S(2)}) %all-to-all-start.2) | async-done | bytes 8388640 | tf_op jit(solution)/shard_map/all_to_all | solution.py:29
  299.3 11.3 %pad_maximum_fusion = f32[32,2,24,2048]{3,2,1,0:T(8,128)} fusion(f32[32,2,16,2048]{3,2,1,0:T(8,128)} %all-to-all-done.2, f32[32,2,8,2048]{3,2,1,0:T(8,128)} %all-to-all-done.1), kind=kLoop, calls=%fused_computation.1 | loop fusion | flops 3145728 | bytes 25165824 | tf_op jit(solution)/shard_map/concatenate | solution.py:30
  310.6 11.8 %gather_fusion = f32[768,2048]{1,0:T(8,128)} fusion(f32[1536,2048]{1,0:T(8,128)} %bitcast.91, s32[1024]{0:T(1024)S(1)} %pad_clamp_fusion), kind=kCustom, calls=%fused_computation | custom fusion | bytes 12585984 | tf_op jit(solution)/shard_map/jit(_take)/gather | solution.py:130
  322.4 7.8 %gather.7 = f32[128,6,2048]{2,1,0:T(8,128)} reshape(f32[768,2048]{1,0:T(8,128)} %gather_fusion) | data formatting | bytes 12582912 | tf_op jit(solution)/shard_map/jit(_take)/gather | solution.py:130
  330.3 6.5 %multiply_reduce_fusion = f32[128,2048]{1,0:T(8,128)S(1)} fusion(f32[128,6,2048]{2,1,0:T(8,128)} %gather.7, f32[128,6]{1,0:T(8,128)S(1)} %copy.57, pred[128,6]{1,0:T(8,128)(4,1)S(1)} %copy.51), kind=kLoop, calls=%fused_computation.4 | loop fusion | flops 4456448 | bytes 7343872 | tf_op jit(solution)/shard_map/reduce_sum | solution.py:133
  337.3 47.0 %all_to_all.59 = f32[4,128,2048]{2,1,0:T(8,128)} all-to-all(f32[4,128,2048]{2,1,0:T(8,128)S(1)} %broadcast_in_dim.20), channel_id=1, replica_groups=mesh['expert'=32,'vocab'=4] {'vocab'}, dimensions={0} | all-to-all | bytes 8388608 | tf_op jit(solution)/shard_map/all_to_all | solution.py:35
  384.3 3.6 reduce_sum.80
  392.5 19.9 %all-to-all-start.6 = ((s32[32,1,128]{2,1,0:T(1,128)}), s32[32,1,128]{2,1,0:T(1,128)S(1)}, u32[]{:S(2)}, u32[]{:S(2)}) async-start(s32[32,1,128]{2,1,0:T(1,128)} %stack.2), calls=%async_computation.6 | async-start | bytes 32768 | tf_op jit(solution)/shard_map/all_to_all | solution.py:144
  412.4 64.2 %all-gather.2.cloned.1.call-done = bf16[4096,2048]{1,0:T(8,128)(2,1)} async-done(((bf16[128,2048]{1,0:T(8,128)(2,1)}), bf16[4096,2048]{1,0:T(8,128)(2,1)}) %all-gather.2.cloned.1.call-update) | async-done | bytes 16777232 | tf_op jit(solution)/shard_map/all_gather | solution.py:142
  476.6 20.1 %fusion.33 = (f32[4096]{0:T(1024)}, f32[4096,768]{0,1:T(8,128)}) fusion(bf16[4096,2048]{1,0:T(8,128)(2,1)} %all-gather.2.cloned.1.call-done, bf16[2048,768]{1,0:T(8,128)(2,1)S(1)} %copy-done), kind=kOutput, calls=%fused_computation.55 | convolution fusion | flops 12888043520 | bytes 32522240 | tf_op jit(solution)/shard_map/dot_general | solution.py:146
  496.7 5.4 all-to-all-start.4
  502.1 7.2 %exponential_reduce_fusion = (f32[4096]{0:T(1024)}, f32[4096]{0:T(1024)}) fusion(f32[4096,768]{0,1:T(8,128)} %get-tuple-element.15, f32[4096]{0:T(1024)} %get-tuple-element.14, s32[4096]{0:T(1024)S(1)} %bitcast.96, s32[768]{0:T(1024)S(1)} %iota_add_fusion), kind=kLoop, calls=%fused_computation.3 | loop fusion | flops 15720448 | bytes 12651520 | tf_op jit(solution)/shard_map/reduce_sum | solution.py:88
  509.5 7.2 %all-to-all-start.5 = ((f32[32,128,1]{1,2,0:T(1,128)}), f32[32,128,1]{1,2,0:T(1,128)S(1)}, u32[]{:S(2)}, u32[]{:S(2)}) async-start(f32[32,128,1]{1,2,0:T(1,128)} %bitcast.16), calls=%async_computation.5 | async-start | bytes 32768 | tf_op jit(solution)/shard_map/all_to_all | solution.py:151
  516.7 7.3 %all-to-all-done.5 = f32[32,128,1]{1,2,0:T(1,128)S(1)} async-done(((f32[32,128,1]{1,2,0:T(1,128)}), f32[32,128,1]{1,2,0:T(1,128)S(1)}, u32[]{:S(2)}, u32[]{:S(2)}) %all-to-all-start.5) | async-done | bytes 16416 | tf_op jit(solution)/shard_map/all_to_all | solution.py:151
  524.1 3.8 all-to-all-start.7
  527.9 7.3 %all-to-all-done.7 = f32[32,128,1]{1,2,0:T(1,128)S(1)} async-done(((f32[32,128,1]{1,2,0:T(1,128)}), f32[32,128,1]{1,2,0:T(1,128)S(1)}, u32[]{:S(2)}, u32[]{:S(2)}) %all-to-all-start.7) | async-done | bytes 16416 | tf_op jit(solution)/shard_map/all_to_all | solution.py:152
  535.3 9.4 %all_to_all.60 = f32[4,3,128]{2,1,0:T(4,128)S(1)} all-to-all(f32[4,3,128]{2,1,0:T(4,128)S(1)} %broadcast_in_dim.22), channel_id=1, replica_groups=mesh['expert'=32,'vocab'=4] {'vocab'}, dimensions={0} | all-to-all | bytes 12288 | tf_op jit(solution)/shard_map/all_to_all | solution.py:35
  (64 shorter events, 25.1 us)
Async XLA Ops:
  6.5 470.0 %copy-start = (bf16[2048,768]{1,0:T(8,128)(2,1)S(1)}, bf16[2048,768]{1,0:T(8,128)(2,1)}, u32[]{:S(2)}) copy-start(bf16[2048,768]{1,0:T(8,128)(2,1)} %param.16) | copy-start | bytes 9437188
  14.6 84.1 %copy-start.6 = (bf16[2,2048,352]{1,2,0:T(8,128)(2,1)S(1)}, bf16[2,2048,352]{1,2,0:T(8,128)(2,1)}, u32[]{:S(2)}) copy-start(bf16[2,2048,352]{1,2,0:T(8,128)(2,1)} %param.12) | copy-start | bytes 8650756
  96.1 2.6 copy-start.1
  117.1 2.2 slice-start
  121.5 57.4 %all-to-all-start.1 = ((f32[32,2,8,2048]{3,2,1,0:T(8,128)}), f32[32,2,8,2048]{3,2,1,0:T(8,128)}, u32[]{:S(2)}, u32[]{:S(2)}) async-start(f32[32,2,8,2048]{3,2,1,0:T(8,128)} %copy.54), calls=%async_computation.1 | async-start | bytes 8388608 | tf_op jit(solution)/shard_map/all_to_all | solution.py:29
  126.4 3.4 slice-start.1
  133.6 52.2 %copy-start.2 = (s32[128,6]{0,1:T(8,128)S(1)}, s32[128,6]{0,1:T(8,128)}, u32[]{:S(2)}) copy-start(s32[128,6]{0,1:T(8,128)} %param.10) | copy-start | bytes 9220
  133.6 52.7 %copy-start.4 = (f32[128,6]{0,1:T(8,128)S(1)}, f32[128,6]{0,1:T(8,128)}, u32[]{:S(2)}) copy-start(f32[128,6]{0,1:T(8,128)} %param.11) | copy-start | bytes 9220
  178.9 120.3 %all-to-all-start.2 = ((f32[32,2,16,2048]{3,2,1,0:T(8,128)}), f32[32,2,16,2048]{3,2,1,0:T(8,128)}, u32[]{:S(2)}, u32[]{:S(2)}) async-start(f32[32,2,16,2048]{3,2,1,0:T(8,128)} %copy.55), calls=%async_computation.2 | async-start | bytes 16777216 | tf_op jit(solution)/shard_map/all_to_all | solution.py:29
  185.8 290.8 %all-gather.2.cloned.1.call-start = ((), (), s32[]{:S(2)}) async-start(), calls=%async_computation.9 | async-start | bytes 17301504 | tf_op jit(solution)/shard_map/all_gather | solution.py:142
  337.3 52.2 %copy-start.3 = (f32[2048]{0:T(1024)S(1)}, f32[2048]{0:T(1024)}, u32[]{:S(2)}) copy-start(f32[2048]{0:T(1024)} %param.15) | copy-start | bytes 24580
  384.3 7.5 %copy-start.5 = (s32[128]{0:T(128)S(1)}, s32[128]{0:T(128)}, u32[]{:S(2)}) copy-start(s32[128]{0:T(128)} %param.17) | copy-start | bytes 1540
  392.5 104.2 %all-to-all-start.6 = ((s32[32,1,128]{2,1,0:T(1,128)}), s32[32,1,128]{2,1,0:T(1,128)S(1)}, u32[]{:S(2)}, u32[]{:S(2)}) async-start(s32[32,1,128]{2,1,0:T(1,128)} %stack.2), calls=%async_computation.6 | async-start | bytes 32768 | tf_op jit(solution)/shard_map/all_to_all | solution.py:144
  496.7 12.8 %all-to-all-start.4 = ((f32[32,128,1]{1,2,0:T(1,128)}), f32[32,128,1]{1,2,0:T(1,128)S(1)}, u32[]{:S(2)}, u32[]{:S(2)}) async-start(f32[32,128,1]{1,2,0:T(1,128)} %bitcast.14), calls=%async_computation.4 | async-start | bytes 32768 | tf_op jit(solution)/shard_map/all_to_all | solution.py:150
  509.5 14.6 %all-to-all-start.5 = ((f32[32,128,1]{1,2,0:T(1,128)}), f32[32,128,1]{1,2,0:T(1,128)S(1)}, u32[]{:S(2)}, u32[]{:S(2)}) async-start(f32[32,128,1]{1,2,0:T(1,128)} %bitcast.16), calls=%async_computation.5 | async-start | bytes 32768 | tf_op jit(solution)/shard_map/all_to_all | solution.py:151
  524.1 11.2 %all-to-all-start.7 = ((f32[32,128,1]{1,2,0:T(1,128)}), f32[32,128,1]{1,2,0:T(1,128)S(1)}, u32[]{:S(2)}, u32[]{:S(2)}) async-start(f32[32,128,1]{1,2,0:T(1,128)} %bitcast.22), calls=%async_computation.7 | async-start | bytes 32768 | tf_op jit(solution)/shard_map/all_to_all | solution.py:152
Sparse Core Ops, SparseCore 0:
  392.0 84.5 all-gather.1
